TPU v7x, 32 devices: a whole 2x2x4 slice. The times are simulated.
32 devices in a mesh: atom: 8 (over z, x), aux: 4 (over y, core).
Axes of the slice: x: 2, y: 2, z: 4, core: 2. Of those that a mesh axis runs over, the one named last changes fastest.
Arguments:
- three_index: bfloat16 [128, 32, 128, 128], P('atom', 'aux'), may hold values from -6 to 6
- pair_mask: int32 [128, 8, 8], P('atom'), may hold values 0 or 1
- pair_owner: int32 [128, 1], P('atom'), may hold values from 0 to 7; in each aligned block of 16 rows (0 to 15, 16 to 31, ...) at most 2 rows name the same one
- pair_sub: int32 [128], P('atom'), may hold values from 0 to 3
- pair_nu: int32 [128], P('atom'), may hold values from 0 to 31
- live_count: int32 [8], P('atom'), may hold values from 1 to 16, 96 in all
- coefficients: bfloat16 [4096, 128], P('atom'), may hold values from -0.5 to 0.5
- fit_matrix: bfloat16 [32, 32], P('aux'), as said below
Outputs:
- exchange: float32 [4096, 4096], P('atom', 'aux')
Inputs may be any that keep to these rules, and one draw needn't show every extreme that they name: `pair_owner`: among the 16 slots of one atom index, at most 2 name the same owner, and in every draw some owner is named exactly 2 times by some atom index's slots. The first live_count[a] slots of atom index a are live; some atom index has all 16 slots live. `fit_matrix`: Symmetric.
All inputs are finite; a program needn't handle non-finite values. No bound on the sum of `pair_mask` or of `live_count` on one device may be relied on, other than what follows from the above.
Results may differ from a plain program's by a relative error of at most 0.012.
Values may be sent and summed in bfloat16 or wider, within the bound.
A program may use at most 128 MiB of HBM per device.

v0:
```python
import jax
import jax.numpy as jnp
from jax import lax
from jax.sharding import PartitionSpec as P

CAP = 2


def per_device(
    three_index, pair_mask, pair_owner, pair_sub, pair_nu, live_count, coefficients, fit_matrix
):
    slot_count, aux_here, block_size, _ = three_index.shape
    rows_here, occupied = coefficients.shape
    blocks_here = rows_here // block_size
    atom_count = lax.axis_size("atom")
    aux_total = fit_matrix.shape[1]
    basis_total = rows_here * atom_count
    shell_size = block_size // pair_mask.shape[1]
    whole_orbitals = lax.all_gather(coefficients, "atom", axis=0, tiled=True)
    orbital_blocks = whole_orbitals.reshape(basis_total // block_size, block_size, occupied)[
        pair_nu
    ]
    expanded = jnp.repeat(jnp.repeat(pair_mask, shell_size, 1), shell_size, 2).astype(jnp.bfloat16)
    masked = three_index * expanded[:, None, :, :]
    halfway = jnp.einsum(
        "tpmn,tni->tpim", masked, orbital_blocks, preferred_element_type=jnp.float32
    )
    alive_mask = jnp.arange(slot_count) < live_count[0]
    halfway = jnp.where(alive_mask[:, None, None, None], halfway, 0.0).astype(jnp.bfloat16)
    owners = pair_owner[:, 0]
    owner_hits = (owners[:, None] == jnp.arange(atom_count)[None, :]).astype(jnp.int32)
    rank_within = jnp.sum(jnp.cumsum(owner_hits, 0) * owner_hits, 1) - 1
    placement = owners * CAP + rank_within
    routing = (jnp.arange(atom_count * CAP)[:, None] == placement[None, :]).astype(jnp.bfloat16)
    outgoing = jnp.dot(routing, halfway.reshape(slot_count, -1), preferred_element_type=jnp.float32)
    outgoing = outgoing.astype(jnp.bfloat16).reshape(
        atom_count, CAP, aux_here, occupied, block_size
    )
    sub_codes = jnp.dot(
        routing, (pair_sub + 1).astype(jnp.bfloat16)[:, None], preferred_element_type=jnp.float32
    )
    sub_codes = sub_codes.astype(jnp.bfloat16).reshape(atom_count, CAP)
    arrived, arrived_codes = (
        lax.all_to_all(outgoing, "atom", split_axis=0, concat_axis=0, tiled=True),
        lax.all_to_all(sub_codes, "atom", split_axis=0, concat_axis=0, tiled=True),
    )
    wanted = (jnp.arange(blocks_here) + 1).astype(jnp.float32)
    selector = (arrived_codes.reshape(1, -1).astype(jnp.float32) == wanted[:, None]).astype(
        jnp.bfloat16
    )
    gathered_rows = jnp.einsum(
        "sc,cpib->pisb",
        selector,
        arrived.reshape(atom_count * CAP, aux_here, occupied, block_size),
        preferred_element_type=jnp.float32,
    )
    local_rows = gathered_rows.reshape(aux_here, occupied, rows_here).astype(jnp.bfloat16)
    fitted_sum = jnp.einsum(
        "qp,pir->qir",
        fit_matrix,
        lax.all_gather(local_rows, "aux", axis=0, tiled=True),
        preferred_element_type=jnp.float32,
    )
    fitted = fitted_sum.astype(jnp.bfloat16)
    partial_value = lax.dot_general(
        local_rows,
        lax.all_gather(fitted, "atom", axis=2, tiled=True),
        (((0, 1), (0, 1)), ((), ())),
        preferred_element_type=jnp.float32,
    )
    column_part = lax.psum_scatter(
        partial_value.astype(jnp.bfloat16), "aux", scatter_dimension=1, tiled=True
    ).astype(jnp.float32)
    return column_part * (aux_total * occupied) ** (-0.5)


def solution(mesh):
    in_specs = (
        P("atom", "aux", None, None),
        P("atom", None, None),
        P("atom", None),
        P("atom"),
        P("atom"),
        P("atom"),
        P("atom", None),
        P("aux", None),
    )
    out_specs = P("atom", "aux")
    return jax.shard_map(
        per_device, mesh=mesh, in_specs=in_specs, out_specs=out_specs, check_vma=False
    )
```

profile of v0, /device:TPU:0, one launch (start us, length us, event | category | flops | bytes accessed | tf_op | source)
XLA Modules:
  0.0 409.8 jit_solution(733651022336806653)
XLA Ops:
  6.5 0.7 all-gather.4.cloned.1.call-update
  7.3 0.7 fusion.25
  8.0 0.8 select_reduce_fusion
  8.9 0.7 add_add_fusion
  9.5 0.8 fusion.23
  10.3 0.7 all_to_all.12
  11.0 7.3 %all-to-all-start.1 = ((bf16[8,1,2]{2,1,0:T(2,128)(2,1)}), bf16[8,1,2]{2,1,0:T(2,128)(2,1)S(1)}, u32[]{:S(2)}, u32[]{:S(2)}) async-start(bf16[8,1,2]{2,1,0:T(2,128)(2,1)} %all_to_all.12), calls=%async_computation.1 | async-start | bytes 8192 | tf_op jit(solution)/shard_map/all_to_all | solution.py:45
  18.9 0.8 convert_element_type.76
  21.3 31.2 %all-gather.4.cloned.1.call-done = bf16[4096,128]{1,0:T(8,128)(2,1)} async-done(((bf16[512,128]{1,0:T(8,128)(2,1)}), bf16[4096,128]{1,0:T(8,128)(2,1)}) %all-gather.4.cloned.1.call-update) | async-done | bytes 1048592 | tf_op jit(solution)/shard_map/all_gather | solution.py:19
  52.5 1.9 gather_fusion
  54.4 4.1 select_convert_fusion
  58.4 2.5 fusion.12
  61.0 2.7 copy.31
  63.7 4.5 %all-to-all-start = ((bf16[8,2,8,128,128]{4,3,2,1,0:T(8,128)(2,1)}), bf16[8,2,8,128,128]{4,3,2,1,0:T(8,128)(2,1)}, u32[]{:S(2)}, u32[]{:S(2)}) async-start(bf16[8,2,8,128,128]{4,3,2,1,0:T(8,128)(2,1)} %bitcast.52), calls=%async_computation | async-start | bytes 8388608 | tf_op jit(solution)/shard_map/all_to_all | solution.py:44
  68.6 91.4 %all-to-all-done = bf16[8,2,8,128,128]{4,3,2,1,0:T(8,128)(2,1)} async-done(((bf16[8,2,8,128,128]{4,3,2,1,0:T(8,128)(2,1)}), bf16[8,2,8,128,128]{4,3,2,1,0:T(8,128)(2,1)}, u32[]{:S(2)}, u32[]{:S(2)}) %all-to-all-start) | async-done | bytes 4194336 | tf_op jit(solution)/shard_map/all_to_all | solution.py:44
  160.0 6.5 %copy.20 = bf16[8,2,8,128,128]{4,1,0,3,2:T(2,128)(2,1)S(1)} copy(bf16[8,2,8,128,128]{4,3,2,1,0:T(8,128)(2,1)} %all-to-all-done) | data formatting | bytes 8388608 | tf_op jit(solution)/shard_map/all_to_all | solution.py:44
  166.5 0.8 fusion.19
  167.3 1.2 convert_element_type.89
  168.6 33.6 %all-gather.6.cloned.1.call-done = bf16[32,128,512]{2,1,0:T(8,128)(2,1)} async-done(((bf16[8,128,512]{2,1,0:T(8,128)(2,1)}), bf16[32,128,512]{2,1,0:T(8,128)(2,1)}) %all-gather.6.cloned.1.call-update) | async-done | bytes 4194320 | tf_op jit(solution)/shard_map/all_gather | solution.py:61
  202.2 5.6 %fusion.20 = bf16[8,128,512]{2,0,1:T(8,128)(2,1)} fusion(bf16[32,128,512]{2,1,0:T(8,128)(2,1)} %all-gather.6.cloned.1.call-done, bf16[8,32]{1,0:T(8,128)(2,1)S(1)} %copy-done), kind=kOutput, calls=%fused_computation.18 | convolution fusion | flops 34078720 | bytes 5243392 | tf_op jit(solution)/shard_map/qp,pir->qir/dot_general | solution.py:58
  208.1 124.8 %all-gather.8.cloned.1.call-done = bf16[8,128,4096]{2,0,1:T(8,128)(2,1)} async-done(((bf16[8,128,512]{2,0,1:T(8,128)(2,1)}), bf16[8,128,4096]{2,0,1:T(8,128)(2,1)}) %all-gather.8.cloned.1.call-update) | async-done | bytes 8388624 | tf_op jit(solution)/shard_map/all_gather | solution.py:67
  332.9 24.8 %bitcast_convert_fusion = bf16[512,4096]{1,0:T(8,128)(2,1)} fusion(bf16[8,128,512]{2,1,0:T(8,128)(2,1)S(1)} %copy-done.1, bf16[8,128,4096]{2,0,1:T(8,128)(2,1)} %all-gather.8.cloned.1.call-done), kind=kOutput, calls=%fused_computation.2 | convolution fusion | flops 4297064448 | bytes 13631488 | tf_op jit(solution)/shard_map/dot_general | solution.py:65
  357.7 42.8 %reduce-scatter.2.cloned.1.call-done = bf16[512,1024]{1,0:T(8,128)(2,1)} async-done(((bf16[512,4096]{1,0:T(8,128)(2,1)}), bf16[512,1024]{1,0:T(8,128)(2,1)}) %reduce-scatter.2.cloned.1.call-update) | async-done | bytes 1048592 | tf_op jit(solution)/shard_map/reduce_scatter | solution.py:71
  400.5 2.8 convert_multiply_fusion
  (24 shorter events, 2.3 us)
Async XLA Ops:
  6.5 195.6 %copy-start = (bf16[8,32]{1,0:T(8,128)(2,1)S(1)}, bf16[8,32]{1,0:T(8,128)(2,1)}, u32[]{:S(2)}) copy-start(bf16[8,32]{1,0:T(8,128)(2,1)} %param.15) | copy-start | bytes 1540
  6.5 46.0 %all-gather.4.cloned.1.call-start = ((), (), s32[]{:S(2)}) async-start(), calls=%async_computation.3 | async-start | bytes 1179648 | tf_op jit(solution)/shard_map/all_gather | solution.py:19
  11.0 52.7 %all-to-all-start.1 = ((bf16[8,1,2]{2,1,0:T(2,128)(2,1)}), bf16[8,1,2]{2,1,0:T(2,128)(2,1)S(1)}, u32[]{:S(2)}, u32[]{:S(2)}) async-start(bf16[8,1,2]{2,1,0:T(2,128)(2,1)} %all_to_all.12), calls=%async_computation.1 | async-start | bytes 8192 | tf_op jit(solution)/shard_map/all_to_all | solution.py:45
  63.7 96.3 %all-to-all-start = ((bf16[8,2,8,128,128]{4,3,2,1,0:T(8,128)(2,1)}), bf16[8,2,8,128,128]{4,3,2,1,0:T(8,128)(2,1)}, u32[]{:S(2)}, u32[]{:S(2)}) async-start(bf16[8,2,8,128,128]{4,3,2,1,0:T(8,128)(2,1)} %bitcast.52), calls=%async_computation | async-start | bytes 8388608 | tf_op jit(solution)/shard_map/all_to_all | solution.py:44
  68.3 133.9 %all-gather.6.cloned.1.call-start = ((), (), s32[]{:S(2)}) async-start(), calls=%async_computation.4 | async-start | bytes 5242880 | tf_op jit(solution)/shard_map/all_gather | solution.py:61
  168.5 164.4 %copy-start.1 = (bf16[8,128,512]{2,1,0:T(8,128)(2,1)S(1)}, bf16[8,128,512]{2,1,0:T(8,128)(2,1)}, u32[]{:S(2)}) copy-start(bf16[8,128,512]{2,1,0:T(8,128)(2,1)} %convert_element_type.89) | copy-start | bytes 3145732
  168.5 164.4 %all-gather.8.cloned.1.call-start = ((), (), s32[]{:S(2)}) async-start(), calls=%async_computation.5 | async-start | bytes 9437184 | tf_op jit(solution)/shard_map/all_gather | solution.py:67
  207.8 192.7 %reduce-scatter.2.cloned.1.call-start = ((), (), s32[]{:S(2)}) async-start(), calls=%async_computation.6 | async-start | bytes 5242880 | tf_op jit(solution)/shard_map/reduce_scatter | solution.py:71
Sparse Core Ops, SparseCore 0:
  9.5 42.9 all-gather.3
  168.7 33.4 all-gather.5
  207.9 124.9 all-gather.7
  357.8 42.5 reduce-scatter.1
where the time goes:
time: 410 us
  waiting for transfers between devices  325 us (79%)
  matrix products  38.5 us (9%)
  local copies, waits for them, and re-layouts  14 us (3%)
  between operations  13.9 us (3%)
  starting transfers between devices  12.4 us (3%)
  other arithmetic  6.54 us (2%)
    all_gather x1, waiting for transfers between devices, per_device(): lax.all_gather(fitted, 'atom', axis=2, tiled=True)  125 us
    all_to_all x1, waiting for transfers between devices, per_device(): lax.all_to_all(outgoing, 'atom', split_axis=0, concat_axis=0, tiled=True)  91.4 us
    reduce_scatter x1, waiting for transfers between devices, per_device(): lax.psum_scatter(partial_value.astype(jnp.bfloat16), 'aux', scatter_dimen...  42.8 us
    all_gather x1, waiting for transfers between devices, per_device(): lax.all_gather(local_rows, 'aux', axis=0, tiled=True)  33.6 us
    all_gather x1, waiting for transfers between devices, per_device(): whole_orbitals = lax.all_gather(coefficients, 'atom', axis=0, tiled=True)  31.2 us
    dot_general x1, matrix products, per_device(): lax.dot_general(local_rows, lax.all_gather(fitted, 'atom', axis=2, tiled=...  24.8 us
  transfers between devices with their start and end apart: 6, of which 5 were waited for; matrix products, arithmetic and copies ran while one was open for 4% of the time, Pallas kernels for 0%

commit v1 on v0

--- a/solution.py
+++ b/solution.py
@@ -55,12 +55,38 @@
         preferred_element_type=jnp.float32,
     )
     local_rows = gathered_rows.reshape(aux_here, occupied, rows_here).astype(jnp.bfloat16)
-    fitted_sum = jnp.einsum(
+    size, place, width = (lax.axis_size("aux"), lax.axis_index("aux"), local_rows.shape[0])
+    right = [(i, (i + 1) % size) for i in range(size)]
+    backward = [(i, (i - 1) % size) for i in range(size)]
+    halfway_2 = size // 2
+    from_left = from_right = local_rows
+    total = jnp.einsum(
         "qp,pir->qir",
-        fit_matrix,
-        lax.all_gather(local_rows, "aux", axis=0, tiled=True),
+        lax.dynamic_slice_in_dim(fit_matrix, place * width, local_rows.shape[0], axis=1),
+        local_rows,
         preferred_element_type=jnp.float32,
     )
+    for lap in range(1, halfway_2 + 1):
+        from_left = lax.ppermute(from_left, "aux", right)
+        if lap < size - halfway_2:
+            from_right = lax.ppermute(from_right, "aux", backward)
+            total = total + jnp.einsum(
+                "qp,pir->qir",
+                lax.dynamic_slice_in_dim(
+                    fit_matrix, (place + lap) % size * width, from_right.shape[0], axis=1
+                ),
+                from_right,
+                preferred_element_type=jnp.float32,
+            )
+        total = total + jnp.einsum(
+            "qp,pir->qir",
+            lax.dynamic_slice_in_dim(
+                fit_matrix, (place - lap) % size * width, from_left.shape[0], axis=1
+            ),
+            from_left,
+            preferred_element_type=jnp.float32,
+        )
+    fitted_sum = total
     fitted = fitted_sum.astype(jnp.bfloat16)
     partial_value = lax.dot_general(
         local_rows,

time: 410 us -> 413 us (level)
    ppermute x0 -> x3, waiting for transfers between devices: none -> 34.6 us  [the longest x2 34.6 us: per_device(): from_left = lax.ppermute(from_left, 'aux', right)]
    all_gather x1 -> x0, waiting for transfers between devices: 33.6 us -> none  [per_device(): lax.all_gather(local_rows, 'aux', axis=0, tiled=True)]
  transfers between devices with their start and end apart: 6 -> 8, of which waited for: 5 -> 6; matrix products, arithmetic and copies ran while one was open for 4% -> 4% of each run, Pallas kernels for 0% -> 0%
where the time goes in v1:
time: 413 us; the launch traced here: 412 us
  waiting for transfers between devices  325 us (79%)
  matrix products  37.4 us (9%)
  local copies, waits for them, and re-layouts  14.8 us (4%)
  starting transfers between devices  14.2 us (3%)
  between operations  13.9 us (3%)
  other arithmetic  6.54 us (2%)
    all_gather x1, waiting for transfers between devices, per_device(): lax.all_gather(fitted, 'atom', axis=2, tiled=True)  125 us
    all_to_all x1, waiting for transfers between devices, per_device(): lax.all_to_all(outgoing, 'atom', split_axis=0, concat_axis=0, tiled=True)  91.4 us
    reduce_scatter x1, waiting for transfers between devices, per_device(): lax.psum_scatter(partial_value.astype(jnp.bfloat16), 'aux', scatter_dimen...  42.7 us
    ppermute x2, waiting for transfers between devices, per_device(): from_left = lax.ppermute(from_left, 'aux', right)  34.6 us
    all_gather x1, waiting for transfers between devices, per_device(): whole_orbitals = lax.all_gather(coefficients, 'atom', axis=0, tiled=True)  31.2 us
    dot_general x1, matrix products, per_device(): lax.dot_general(local_rows, lax.all_gather(fitted, 'atom', axis=2, tiled=...  24.8 us
  transfers between devices with their start and end apart: 8, of which 6 were waited for; matrix products, arithmetic and copies ran while one was open for 4% of the time, Pallas kernels for 0%

profile of v1, /device:TPU:0, one launch (start us, length us, event | category | flops | bytes accessed | tf_op | source)
XLA Modules:
  0.0 412.2 jit_solution(9965074642656926662)
XLA Ops:
  7.3 0.7 fusion.17
  8.0 0.8 select_reduce_fusion
  9.5 0.8 fusion.15
  11.0 7.3 %all-to-all-start.1 = ((bf16[8,1,2]{2,1,0:T(2,128)(2,1)}), bf16[8,1,2]{2,1,0:T(2,128)(2,1)S(1)}, u32[]{:S(2)}, u32[]{:S(2)}) async-start(bf16[8,1,2]{2,1,0:T(2,128)(2,1)} %all_to_all.12), calls=%async_computation.1 | async-start | bytes 8192 | tf_op jit(solution)/shard_map/all_to_all | solution.py:45
  18.9 0.8 convert_element_type.73
  21.3 31.2 %all-gather.3.cloned.1.call-done = bf16[4096,128]{1,0:T(8,128)(2,1)} async-done(((bf16[512,128]{1,0:T(8,128)(2,1)}), bf16[4096,128]{1,0:T(8,128)(2,1)}) %all-gather.3.cloned.1.call-update) | async-done | bytes 1048592 | tf_op jit(solution)/shard_map/all_gather | solution.py:19
  52.5 1.9 gather_fusion
  54.4 4.1 select_convert_fusion
  58.4 2.5 fusion.10
  61.0 2.8 copy.33
  63.7 4.5 %all-to-all-start = ((bf16[8,2,8,128,128]{4,3,2,1,0:T(8,128)(2,1)}), bf16[8,2,8,128,128]{4,3,2,1,0:T(8,128)(2,1)}, u32[]{:S(2)}, u32[]{:S(2)}) async-start(bf16[8,2,8,128,128]{4,3,2,1,0:T(8,128)(2,1)} %bitcast.62), calls=%async_computation | async-start | bytes 8388608 | tf_op jit(solution)/shard_map/all_to_all | solution.py:44
  68.6 91.4 %all-to-all-done = bf16[8,2,8,128,128]{4,3,2,1,0:T(8,128)(2,1)} async-done(((bf16[8,2,8,128,128]{4,3,2,1,0:T(8,128)(2,1)}), bf16[8,2,8,128,128]{4,3,2,1,0:T(8,128)(2,1)}, u32[]{:S(2)}, u32[]{:S(2)}) %all-to-all-start) | async-done | bytes 4194336 | tf_op jit(solution)/shard_map/all_to_all | solution.py:44
  160.0 6.5 %copy.20 = bf16[8,2,8,128,128]{4,1,0,3,2:T(2,128)(2,1)S(1)} copy(bf16[8,2,8,128,128]{4,3,2,1,0:T(8,128)(2,1)} %all-to-all-done) | data formatting | bytes 8388608 | tf_op jit(solution)/shard_map/all_to_all | solution.py:44
  166.5 0.8 fusion.14
  167.7 1.5 copy.22
  169.3 1.7 collective-permute-start
  171.0 22.2 %collective-permute-done.1 = bf16[8,128,512]{2,0,1:T(8,128)(2,1)S(1)} collective-permute-done((bf16[8,128,512]{2,0,1:T(8,128)(2,1)}, bf16[8,128,512]{2,0,1:T(8,128)(2,1)S(1)}, u32[]{:S(2)}, u32[]{:S(2)}) %collective-permute-start.1) | collective-permute-done | bytes 1048608 | tf_op jit(solution)/shard_map/ppermute | solution.py:70
  193.3 0.7 fusion.25
  195.1 12.5 %collective-permute-done.2 = bf16[8,128,512]{2,0,1:T(8,128)(2,1)} collective-permute-done((bf16[8,128,512]{2,0,1:T(8,128)(2,1)S(1)}, bf16[8,128,512]{2,0,1:T(8,128)(2,1)}, u32[]{:S(2)}, u32[]{:S(2)}) %collective-permute-start.2) | collective-permute-done | bytes 1048608 | tf_op jit(solution)/shard_map/ppermute | solution.py:70
  207.5 2.8 add_convert_fusion
  210.6 124.8 %all-gather.5.cloned.1.call-done = bf16[8,128,4096]{2,0,1:T(8,128)(2,1)} async-done(((bf16[8,128,512]{2,0,1:T(8,128)(2,1)}), bf16[8,128,4096]{2,0,1:T(8,128)(2,1)}) %all-gather.5.cloned.1.call-update) | async-done | bytes 8388624 | tf_op jit(solution)/shard_map/all_gather | solution.py:93
  335.4 24.8 %bitcast_convert_fusion = bf16[512,4096]{1,0:T(8,128)(2,1)} fusion(bf16[8,128,512]{2,1,0:T(8,128)(2,1)S(1)} %convert_element_type.86, bf16[8,128,4096]{2,0,1:T(8,128)(2,1)} %all-gather.5.cloned.1.call-done), kind=kOutput, calls=%fused_computation.2 | convolution fusion | flops 4297064448 | bytes 13631488 | tf_op jit(solution)/shard_map/dot_general | solution.py:91
  360.2 42.7 %reduce-scatter.2.cloned.1.call-done = bf16[512,1024]{1,0:T(8,128)(2,1)} async-done(((bf16[512,4096]{1,0:T(8,128)(2,1)}), bf16[512,1024]{1,0:T(8,128)(2,1)}) %reduce-scatter.2.cloned.1.call-update) | async-done | bytes 1048592 | tf_op jit(solution)/shard_map/reduce_scatter | solution.py:97
  402.9 2.8 convert_multiply_fusion
  (29 shorter events, 5.8 us)
Async XLA Ops:
  6.5 186.8 %copy-start = (bf16[8,32]{1,0:T(8,128)(2,1)S(1)}, bf16[8,32]{1,0:T(8,128)(2,1)}, u32[]{:S(2)}) copy-start(bf16[8,32]{1,0:T(8,128)(2,1)} %param.15) | copy-start | bytes 1540
  6.5 46.0 %all-gather.3.cloned.1.call-start = ((), (), s32[]{:S(2)}) async-start(), calls=%async_computation.3 | async-start | bytes 1179648 | tf_op jit(solution)/shard_map/all_gather | solution.py:19
  11.0 52.7 %all-to-all-start.1 = ((bf16[8,1,2]{2,1,0:T(2,128)(2,1)}), bf16[8,1,2]{2,1,0:T(2,128)(2,1)S(1)}, u32[]{:S(2)}, u32[]{:S(2)}) async-start(bf16[8,1,2]{2,1,0:T(2,128)(2,1)} %all_to_all.12), calls=%async_computation.1 | async-start | bytes 8192 | tf_op jit(solution)/shard_map/all_to_all | solution.py:45
  63.7 96.3 %all-to-all-start = ((bf16[8,2,8,128,128]{4,3,2,1,0:T(8,128)(2,1)}), bf16[8,2,8,128,128]{4,3,2,1,0:T(8,128)(2,1)}, u32[]{:S(2)}, u32[]{:S(2)}) async-start(bf16[8,2,8,128,128]{4,3,2,1,0:T(8,128)(2,1)} %bitcast.62), calls=%async_computation | async-start | bytes 8388608 | tf_op jit(solution)/shard_map/all_to_all | solution.py:44
  68.3 267.1 %all-gather.5.cloned.1.call-start = ((), (), s32[]{:S(2)}) async-start(), calls=%async_computation.4 | async-start | bytes 9437184 | tf_op jit(solution)/shard_map/all_gather | solution.py:93
  169.3 23.9 %collective-permute-start.1 = (bf16[8,128,512]{2,0,1:T(8,128)(2,1)}, bf16[8,128,512]{2,0,1:T(8,128)(2,1)S(1)}, u32[]{:S(2)}, u32[]{:S(2)}) collective-permute-start(bf16[8,128,512]{2,0,1:T(8,128)(2,1)} %copy.22), channel_id=1, source_target_pairs={{0,1},{1,2},{2,3},{3,0},{4,5},{5,6},{6,7},{7,4},{8,9},{9,10},{10,1... | collective-permute-start | bytes 3145736 | tf_op jit(solution)/shard_map/ppermute | solution.py:70
  169.3 25.3 %collective-permute-start = (bf16[8,128,512]{2,0,1:T(8,128)(2,1)}, bf16[8,128,512]{2,0,1:T(8,128)(2,1)S(1)}, u32[]{:S(2)}, u32[]{:S(2)}) collective-permute-start(bf16[8,128,512]{2,0,1:T(8,128)(2,1)} %copy.22), channel_id=1, source_target_pairs={{0,3},{1,0},{2,1},{3,2},{4,7},{5,4},{6,5},{7,6},{8,11},{9,8},{10,9... | collective-permute-start | bytes 3145736 | tf_op jit(solution)/shard_map/ppermute | solution.py:72
  193.2 14.3 %collective-permute-start.2 = (bf16[8,128,512]{2,0,1:T(8,128)(2,1)S(1)}, bf16[8,128,512]{2,0,1:T(8,128)(2,1)}, u32[]{:S(2)}, u32[]{:S(2)}) collective-permute-start(bf16[8,128,512]{2,0,1:T(8,128)(2,1)S(1)} %collective-permute-done.1), channel_id=1, source_target_pairs={{0,1},{1,2},{2,3},{3,0},{4,5},{5,6},{6,7},{7,4},{8,9},{9,10},{10,1... | collective-permute-start | bytes 3145736 | tf_op jit(solution)/shard_map/ppermute | solution.py:70
  210.3 192.6 %reduce-scatter.2.cloned.1.call-start = ((), (), s32[]{:S(2)}) async-start(), calls=%async_computation.5 | async-start | bytes 5242880 | tf_op jit(solution)/shard_map/reduce_scatter | solution.py:97
Sparse Core Ops, SparseCore 0:
  9.5 42.9 all-gather.2
  210.4 124.8 all-gather.4
  360.3 42.5 reduce-scatter.1
